TPU v7x, 128 devices: a whole 4x4x4 slice. The times are simulated.
128 devices in a mesh: row: 8 (over z_lo, x), col: 16 (over y, z_hi, core).
Axes of the slice: x: 4, y: 4, z: 4 (z_hi: 2, z_lo: 2; z = z_hi * 2 + z_lo), core: 2. Of those that a mesh axis runs over, the one named last changes fastest.
Arguments:
- amplitudes: bfloat16 [4096, 16384], P('row', 'col'), may hold values from -6 to 6
- integrals: bfloat16 [16384, 16384], P('col')
- block_irrep: int32 [64], replicated, may hold values from 0 to 3, as said below
- irrep_size: int32 [4], replicated, may hold values from 64 to 256
- partner: int32 [64], replicated, may hold values from 0 to 63, as said below
Outputs:
- residual: bfloat16 [4096, 16384], P('row', 'col')
Inputs may be any that keep to these rules, and one draw needn't show every extreme that they name: partner is an involution on the 64 blocks without fixed blocks; a block and its partner have the same position among the 4 blocks of their col indices, and the blocks of one col index have partners at 4 different other col indices. `block_irrep`: a block and its partner have the same irrep.
All inputs are finite; a program needn't handle non-finite values.
Results may differ from a plain program's by a relative error of at most 0.0051.
Values may be sent and summed in bfloat16 or wider, within the bound.
A program may use at most 256 MiB of HBM per device.

v0:
```python
import jax
import jax.numpy as jnp
from jax import lax
from jax.sharding import PartitionSpec as P

BW = 256
NIRREP = 4
BPC = 4
O_DEV = 8


def body(amplitudes, integrals, block_irrep, irrep_size, partner):
    row_count = lax.axis_size("row")
    col_pos = lax.axis_index("col")
    pair_rows, local_width = amplitudes.shape
    blocks = block_irrep.shape[0]
    total_width = blocks * BW
    choose = (block_irrep[:, None] == jnp.arange(NIRREP, dtype=jnp.int32)[None, :]).astype(
        jnp.int32
    )
    block_size = jnp.sum(choose * irrep_size[None, :], axis=1)
    live_all = jnp.arange(BW, dtype=jnp.int32)[None, :] < block_size[:, None]
    own_live = lax.dynamic_slice_in_dim(live_all, col_pos * BPC, BPC, 0).reshape(local_width)
    masked_amp = amplitudes * own_live.astype(jnp.bfloat16)[None, :]
    own_irrep = lax.dynamic_slice_in_dim(block_irrep, col_pos * BPC, BPC, 0)
    allowed = (own_irrep[:, None] == block_irrep[None, :]).astype(jnp.bfloat16)
    masked_int = (integrals.reshape(BPC, BW, blocks, BW) * allowed[:, None, :, None]).reshape(
        local_width, total_width
    )
    summed = lax.dot_general(
        lax.all_gather(masked_amp, "col", axis=1, tiled=True),
        masked_int,
        (((1,), (1,)), ((), ())),
        preferred_element_type=jnp.float32,
    )
    ladder = summed.astype(jnp.bfloat16)
    arranged = ladder.reshape(O_DEV, row_count, O_DEV, local_width)
    swapped = lax.all_to_all(arranged, "row", split_axis=1, concat_axis=1, tiled=True)
    flipped = jnp.transpose(swapped, (2, 1, 0, 3)).reshape(pair_rows, local_width)
    own_partner = lax.dynamic_slice_in_dim(partner, col_pos * BPC, BPC, 0)
    everything = lax.all_gather(flipped, "col", axis=1, tiled=True)
    fetched = jnp.take(everything.reshape(pair_rows, blocks, BW), own_partner, axis=1)
    combined = ladder.astype(jnp.float32) + fetched.reshape(pair_rows, local_width).astype(
        jnp.float32
    )
    return (combined * own_live.astype(jnp.float32)[None, :]).astype(jnp.bfloat16)


def solution(mesh):
    in_specs = (P("row", "col"), P("col", None), P(), P(), P())
    out_specs = P("row", "col")
    return jax.shard_map(body, mesh=mesh, in_specs=in_specs, out_specs=out_specs, check_vma=False)
```

profile of v0, /device:TPU:1, one launch (start us, length us, event | category | flops | bytes accessed | tf_op | source)
XLA Modules:
  0.0 342.2 jit_solution(4698869125359627448)
XLA Ops:
  6.5 0.0 all-gather.3.cloned.1.call-start
  6.5 0.8 select_reduce_fusion
  7.3 0.1 dynamic-slice
  7.4 0.1 fusion.7
  7.5 2.3 broadcast_multiply_fusion
  9.7 0.0 all-gather.3.cloned.1.call-update
  9.7 0.0 all-gather.5.cloned.1.call-start
  9.8 0.7 dynamic_slice.10
  10.5 0.7 compare_convert_fusion
  11.3 11.1 %mul.45 = bf16[4,256,64,256]{3,2,1,0:T(8,128)(2,1)} broadcast(bf16[4,64]{1,0:T(4,128)(2,1)S(1)} %compare_convert_fusion), dimensions={0,2} | broadcast | bytes 33554944 | tf_op jit(solution)/shard_map/mul | solution.py:27
  22.3 31.2 %copy.24 = bf16[128,8,64,256]{3,1,2,0:T(8,128)(2,1)} copy(bf16[128,8,64,256]{3,2,1,0:T(8,128)(2,1)} %bitcast.18) | data formatting | bytes 67108864
  53.5 70.3 %all-gather.3.cloned.1.call-done = bf16[512,16384]{1,0:T(8,128)(2,1)} async-done(((bf16[512,1024]{1,0:T(8,128)(2,1)}), bf16[512,16384]{1,0:T(8,128)(2,1)}) %all-gather.3.cloned.1.call-update) | async-done | bytes 16777232 | tf_op jit(solution)/shard_map/all_gather | solution.py:31
  123.9 0.0 copy-start
  123.9 29.8 %fusion.2 = bf16[512,1024]{1,0:T(8,128)(2,1)S(1)} fusion(bf16[512,16384]{1,0:T(8,128)(2,1)} %all-gather.3.cloned.1.call-done, bf16[1024,16384]{1,0:T(8,128)(2,1)} %param.6, bf16[1024,16384]{1,0:T(8,128)(2,1)} %bitcast.20), kind=kOutput, calls=%fused_computation.4 | convolution fusion | flops 17197170688 | bytes 84934656 | tf_op jit(solution)/shard_map/dot_general | solution.py:30
  153.7 0.6 copy.17
  154.3 19.7 %all_to_all.5 = bf16[8,8,8,1024]{3,0,2,1:T(8,128)(2,1)S(1)} all-to-all(bf16[8,8,8,1024]{3,0,2,1:T(8,128)(2,1)S(1)} %copy.17), channel_id=1, replica_groups=mesh['row'=8,'col'=16] {'row'}, dimensions={1} | all-to-all | bytes 2097152 | tf_op jit(solution)/shard_map/all_to_all | solution.py:38
  174.0 1.1 copy.18
  175.1 0.0 all-gather.5.cloned.1.call-update
  175.1 0.0 copy-done
  175.2 0.1 compare_and_fusion
  175.2 0.1 broadcast_in_dim.26
  175.3 107.3 %all-gather.5.cloned.1.call-done = bf16[512,16384]{1,0:T(8,128)(2,1)} async-done(((bf16[512,1024]{1,0:T(8,128)(2,1)}), bf16[512,16384]{1,0:T(8,128)(2,1)}) %all-gather.5.cloned.1.call-update) | async-done | bytes 16777232 | tf_op jit(solution)/shard_map/all_gather | solution.py:41
  282.7 22.4 %copy.19 = bf16[512,16384]{0,1:T(8,128)(2,1)} copy(bf16[512,16384]{1,0:T(8,128)(2,1)} %all-gather.5.cloned.1.call-done) | data formatting | bytes 33554432 | tf_op jit(solution)/shard_map/all_gather | solution.py:41
  305.1 22.3 %copy.20 = bf16[512,64,256]{2,0,1:T(8,128)(2,1)} copy(bf16[512,64,256]{0,2,1:T(8,128)(2,1)} %bitcast.19) | data formatting | bytes 33554432 | tf_op jit(solution)/shard_map/reshape | solution.py:42
  327.4 6.4 %gather_fusion = bf16[4,512,256]{2,1,0:T(8,128)(2,1)S(1)} fusion(bf16[512,64,256]{2,0,1:T(8,128)(2,1)} %copy.20, s32[1024]{0:T(1024)S(1)} %pad_clamp_fusion), kind=kCustom, calls=%fused_computation | custom fusion | bytes 2097168 | tf_op jit(solution)/shard_map/jit(_take)/gather | solution.py:42
  333.8 0.1 copy.22
  333.9 1.4 multiply_convert_fusion
  (4 shorter events, 0.0 us)
Async XLA Ops:
  6.5 117.3 %all-gather.3.cloned.1.call-start = ((), (), s32[]{:S(2)}) async-start(), calls=%async_computation.1 | async-start | bytes 17825792 | tf_op jit(solution)/shard_map/all_gather | solution.py:31
  9.7 272.9 %all-gather.5.cloned.1.call-start = ((), (), s32[]{:S(2)}) async-start(), calls=%async_computation.2 | async-start | bytes 17825792 | tf_op jit(solution)/shard_map/all_gather | solution.py:41
  123.9 51.3 %copy-start = (s32[64]{0:T(128)S(1)}, s32[64]{0:T(128)}, u32[]{:S(2)}) copy-start(s32[64]{0:T(128)} %param.9) | copy-start | bytes 772
Sparse Core Ops, SparseCore 0:
  9.9 113.9 all-gather.2
  175.3 107.3 all-gather.4
where the time goes:
time: 344 us; the launch traced here: 342 us
  waiting for transfers between devices  178 us (52%)
  local copies, waits for them, and re-layouts  96.1 us (28%)
  matrix products  29.8 us (9%)
  blocking collectives  19.7 us (6%)
  between operations  13.5 us (4%)
  other arithmetic  5.35 us (2%)
    all_gather x1, waiting for transfers between devices, body(): everything = lax.all_gather(flipped, 'col', axis=1, tiled=True)  107 us
    all_gather x1, waiting for transfers between devices, body(): lax.all_gather(masked_amp, 'col', axis=1, tiled=True)  70.3 us
    unnamed x5, local copies, waits for them, and re-layouts  31.2 us
    dot_general x1, matrix products, body(): lax.dot_general(lax.all_gather(masked_amp, 'col', axis=1, tiled=True), ma...  29.8 us
    all_gather x1, local copies, waits for them, and re-layouts, body(): everything = lax.all_gather(flipped, 'col', axis=1, tiled=True)  22.4 us
    reshape x1, local copies, waits for them, and re-layouts, body(): everything.reshape(pair_rows, blocks, BW)  22.3 us
    all_to_all x1, blocking collectives, body(): lax.all_to_all(arranged, 'row', split_axis=1, concat_axis=1, tiled=True)  19.7 us
    mul x1, local copies, waits for them, and re-layouts, body(): integrals.reshape(BPC, BW, blocks, BW) * allowed[:, None, :, None]  11.1 us
  transfers between devices with their start and end apart: 2, of which 2 were waited for; matrix products, arithmetic and copies ran while one was open for 13% of the time, Pallas kernels for 0%

commit v1 on v0

v1 whole, which is shorter than its diff:
```python
import functools

import jax
import jax.numpy as jnp
from jax import lax
from jax.experimental import pallas as pl
from jax.experimental.pallas import tpu as pltpu
from jax.sharding import PartitionSpec as P

MESH = pl.DeviceIdType.MESH
BW = 256
BPC = 4
NOCC = 64
CHUNKS = 2
COLS = 16
ROWS = 8


def one_hot(shape, target):
    row = lax.broadcasted_iota(jnp.int32, shape, 0)
    column = lax.broadcasted_iota(jnp.int32, shape, 1)
    return jnp.where(column == target(row), 1.0, 0.0).astype(jnp.bfloat16)


def kernel(
    irrep, size, partner, amp_hbm, int_hbm, out_ref,
    amp, ints, own, total, ladder, send2, recv2,
    own_sem, int_sem, y_send, y_recv, k_send, k_recv, s1_send, s1_recv, s2_send, s2_recv, *recv1,
):
    rows = amp_hbm.shape[0]
    width = amp_hbm.shape[1]
    part = rows // CHUNKS
    firsts = ROWS // CHUNKS
    piece = part // COLS
    r, c = lax.axis_index("row"), lax.axis_index("col")
    y, zh, k = c // 4, (c // 2) % 2, c % 2

    def col(dy, dz, dk):
        return lax.rem(y + dy, 4) * 4 + lax.rem(zh + dz, 2) * 2 + lax.rem(k + dk, 2)

    up, down, across, twin = (r, col(1, 0, 0)), (r, col(3, 0, 0)), (r, col(0, 1, 0)), (r, col(0, 0, 1))

    own_copy = pltpu.make_async_copy(amp_hbm, own, own_sem)
    own_copy.start()

    barrier = pltpu.get_barrier_semaphore()

    def greet_col(o, carry):
        pl.semaphore_signal(barrier, inc=1, device_id=(r, lax.rem(c + o, COLS)), device_id_type=MESH)
        return carry

    lax.fori_loop(1, COLS, greet_col, 0)

    def group_at(row, s):
        sy, sz, sk = s // 4, (s // 2) % 2, s % 2
        x, z = lax.rem(row % 4 + sy + 2 * sk, 4), lax.rem(row // 4 + sz, 2)
        return (z * 4 + x) * 2 + sk

    def sender(row, slot):
        there, sk = slot // 2, slot % 2
        sz = lax.rem(row // 4 + there // 4, 2)
        sy = lax.rem(row % 4 + 8 - there % 4 - 2 * sk, 4)
        return there, sy * 4 + sz * 2 + sk

    target = group_at(r, c) // 2

    def greet_row(n, carry):
        there, column = sender(r, n)

        @pl.when(jnp.logical_or(there != r, column != c))
        def _():
            pl.semaphore_signal(barrier, inc=1, device_id=(there, column), device_id_type=MESH)

        return carry

    lax.fori_loop(0, 2 * ROWS, greet_row, 0)

    def int_copy(n):
        at = lax.rem(c + n, COLS)
        return pltpu.make_async_copy(
            int_hbm.at[:, pl.ds(pl.multiple_of(at * width, width), width)], ints.at[at], int_sem.at[at]
        )

    def start_int(n, carry):
        int_copy(n).start()
        return carry

    lax.fori_loop(0, COLS, start_int, 0)

    def live_of(base):
        lane = lax.broadcasted_iota(jnp.int32, (1, BW), 1)
        return jnp.concatenate(
            [jnp.where(lane < size[irrep[base + b]], 1.0, 0.0) for b in range(BPC)], axis=1
        )

    live = live_of(c * BPC)

    def natural(n):
        group, rest = n // piece, n % piece
        return (rest // 4) * NOCC + group * 4 + rest % 4

    own_copy.wait()
    arrange = one_hot((part, part), natural)
    for q in range(CHUNKS):
        rearranged = jnp.dot(arrange, own[q * part : (q + 1) * part, :], preferred_element_type=jnp.float32)
        amp[c, q * part : (q + 1) * part, :] = (rearranged * live).astype(jnp.bfloat16)

    pl.semaphore_wait(barrier, COLS - 1 + jnp.where(target == r, 2 * ROWS - 1, 2 * ROWS))

    def move(at, q, start, count, to, sems, n):
        span = pl.ds(q * part + start, count)
        return pltpu.make_async_remote_copy(
            src_ref=amp.at[at, span], dst_ref=amp.at[at, span],
            send_sem=sems[0].at[q, n], recv_sem=sems[1].at[q, n],
            device_id=to, device_id_type=MESH,
        )

    half = part // 2
    ysem, ksem = (y_send, y_recv), (k_send, k_recv)
    started = []

    def go(copy):
        copy.start()
        started.append(copy)

    def send_own(q):
        go(move(c, q, 0, part, up, ysem, 0))
        go(move(c, q, 0, part, down, ysem, 1))
        go(move(c, q, 0, part, across, ysem, 4))
        go(move(c, q, 0, part, twin, ksem, 0))

    def arrived(at, q, start, count, sems, n):
        move(at, q, start, count, up, sems, n).wait_recv()

    def near(q):
        at = col(3, 0, 0)
        arrived(at, q, 0, part, ysem, 0)
        go(move(at, q, 0, half, up, ysem, 2))
        go(move(at, q, 0, part, twin, ksem, 1))
        at = col(1, 0, 0)
        arrived(at, q, 0, part, ysem, 1)
        go(move(at, q, half, half, down, ysem, 3))
        go(move(at, q, 0, part, twin, ksem, 2))

    def over(q):
        at = col(0, 1, 0)
        arrived(at, q, 0, part, ysem, 4)
        go(move(at, q, 0, part, up, ysem, 5))
        go(move(at, q, 0, part, down, ysem, 6))
        go(move(at, q, 0, part, twin, ksem, 3))

    def far(q):
        at = col(2, 0, 0)
        arrived(at, q, 0, half, ysem, 2)
        go(move(at, q, 0, half, across, ysem, 7))
        arrived(at, q, half, half, ysem, 3)
        go(move(at, q, half, half, across, ysem, 8))
        go(move(at, q, 0, part, twin, ksem, 4))

    def near_over(q):
        at = col(3, 1, 0)
        arrived(at, q, 0, part, ysem, 5)
        go(move(at, q, 0, part, twin, ksem, 5))
        at = col(1, 1, 0)
        arrived(at, q, 0, part, ysem, 6)
        go(move(at, q, 0, part, twin, ksem, 6))

    def far_over(q):
        at = col(2, 1, 0)
        arrived(at, q, 0, half, ysem, 7)
        arrived(at, q, half, half, ysem, 8)
        go(move(at, q, 0, part, twin, ksem, 7))

    def mask_ints(n, carry):
        int_copy(n).wait()
        at = lax.rem(c + n, COLS)
        for a in range(BPC):
            for b in range(BPC):
                same = irrep[c * BPC + a] == irrep[at * BPC + b]
                keep = jnp.where(same, 1.0, 0.0).astype(jnp.bfloat16)
                ints[at, a * BW : (a + 1) * BW, b * BW : (b + 1) * BW] *= keep
        return carry

    def multiply(q, at, first=False):
        def block(a, carry):
            span = pl.ds(pl.multiple_of(a * BW, BW), BW)
            product = lax.dot_general(
                amp[at, q * part : (q + 1) * part, :], ints[at, span, :],
                (((1,), (1,)), ((), ())), preferred_element_type=jnp.float32,
            )
            total[q, a] = product if first else total[q, a] + product
            return carry

        lax.fori_loop(0, BPC, block, 0)

    def from_twin(q, n):
        dy, dz = ((0, 0), (3, 0), (1, 0), (0, 1), (2, 0), (3, 1), (1, 1), (2, 1))[n]
        at = col(dy, dz, 1)
        arrived(at, q, 0, part, ksem, n)
        multiply(q, at)

    def step1(q, o):
        to = lax.rem(c + o, COLS)
        return pltpu.make_async_remote_copy(
            src_ref=ladder.at[q, group_at(r, to)], dst_ref=recv1[q].at[c], send_sem=s1_send.at[q, to], recv_sem=s1_recv.at[q, c],
            device_id=(r, to), device_id_type=MESH,
        )

    def exchange1(q):
        for a in range(BPC):
            ladder[q, :, :, a * BW : (a + 1) * BW] = total[q, a].astype(jnp.bfloat16).reshape(COLS, piece, BW)

        def send(o, carry):
            step1(q, o).start()
            return carry

        lax.fori_loop(1, COLS, send, 0)
        recv1[q][c] = ladder[q, group_at(r, c)]

    def step2(q, to, slot):
        return pltpu.make_async_remote_copy(
            src_ref=send2.at[q, to], dst_ref=recv2.at[q, slot], send_sem=s2_send.at[q, to], recv_sem=s2_recv.at[q, slot],
            device_id=(target, to), device_id_type=MESH,
        )

    mine = r * 2 + k

    def exchange2(q):
        def arrive(o, carry):
            at = lax.rem(c + o, COLS)
            pltpu.make_async_remote_copy(
                src_ref=ladder.at[q, at], dst_ref=recv1[q].at[at], send_sem=s1_send.at[q, at], recv_sem=s1_recv.at[q, at],
                device_id=(r, at), device_id_type=MESH,
            ).wait_recv()
            return carry

        lax.fori_loop(1, COLS, arrive, 0)

        def send(o, carry):
            to = lax.rem(c + o, COLS)
            for b in range(BPC):
                source = partner[to * BPC + b] // BPC
                send2[q, to, :, b * BW : (b + 1) * BW] = recv1[q][source, :, b * BW : (b + 1) * BW]

            local = jnp.logical_and(target == r, to == c)

            @pl.when(jnp.logical_not(local))
            def _():
                step2(q, to, mine).start()

            @pl.when(local)
            def _():
                recv2[q, mine] = send2[q, to]

            return carry

        lax.fori_loop(0, COLS, send, 0)

    def exchange2_done(q):
        def arrive(slot, carry):
            there, column = sender(r, slot)

            @pl.when(jnp.logical_or(there != r, column != c))
            def _():
                step2(q, c, slot).wait_recv()

            return carry

        lax.fori_loop(0, 2 * ROWS, arrive, 0)

    def unnatural(m):
        first, second = m // NOCC, m % NOCC
        return (second // 4) * piece + first * 4 + second % 4

    for q in range(CHUNKS):
        send_own(q)
    lax.fori_loop(0, COLS, mask_ints, 0)
    for q in range(CHUNKS):
        multiply(q, c, first=True)
    for q in range(CHUNKS):
        near(q)
        over(q)
        from_twin(q, 0)
    far(0)
    far(1)
    for q in range(CHUNKS):
        multiply(q, col(3, 0, 0))
        multiply(q, col(1, 0, 0))
        multiply(q, col(0, 1, 0))
        from_twin(q, 1)
        from_twin(q, 2)
        from_twin(q, 3)
        multiply(q, col(2, 0, 0))
    near_over(0)
    from_twin(0, 4)
    multiply(0, col(3, 1, 0))
    multiply(0, col(1, 1, 0))
    far_over(0)
    from_twin(0, 5)
    from_twin(0, 6)
    multiply(0, col(2, 1, 0))
    near_over(1)
    from_twin(0, 7)
    exchange1(0)
    from_twin(1, 4)
    multiply(1, col(3, 1, 0))
    multiply(1, col(1, 1, 0))
    far_over(1)
    from_twin(1, 5)
    from_twin(1, 6)
    multiply(1, col(2, 1, 0))
    from_twin(1, 7)
    exchange1(1)
    exchange2(0)
    exchange2(1)
    for q in range(CHUNKS):
        exchange2_done(q)

    back = one_hot((part, part), unnatural)
    for q in range(CHUNKS):
        result = jnp.dot(back, ladder[q].reshape(part, width), preferred_element_type=jnp.float32)
        for p in range(CHUNKS):
            row = lax.broadcasted_iota(jnp.int32, (part, part), 0)
            column = lax.broadcasted_iota(jnp.int32, (part, part), 1)
            slot, rest = column // piece, column % piece
            first = (slot % 2) * 4 + rest % 4
            second = (slot // 2) * ROWS + p * firsts + rest // 4
            fetch = jnp.where(first * NOCC + second == row + q * part, 1.0, 0.0).astype(jnp.bfloat16)
            result += jnp.dot(fetch, recv2[p].reshape(part, width), preferred_element_type=jnp.float32)
        out_ref[q * part : (q + 1) * part, :] = (result * live).astype(jnp.bfloat16)

    for copy in started:
        copy.wait_send()
    for q in range(CHUNKS):

        def sent1(o, carry):
            step1(q, o).wait_send()
            return carry

        lax.fori_loop(1, COLS, sent1, 0)

        def sent2(to, carry):
            @pl.when(jnp.logical_not(jnp.logical_and(target == r, to == c)))
            def _():
                step2(q, to, mine).wait_send()

            return carry

        lax.fori_loop(0, COLS, sent2, 0)


def body(amplitudes, integrals, block_irrep, irrep_size, partner):
    rows, width = amplitudes.shape
    part = rows // CHUNKS
    piece = part // COLS
    dma = pltpu.SemaphoreType.DMA
    return pl.pallas_call(
        kernel,
        out_shape=jax.ShapeDtypeStruct((rows, width), jnp.bfloat16),
        in_specs=[pl.BlockSpec(memory_space=pltpu.SMEM)] * 3 + [pl.BlockSpec(memory_space=pl.ANY)] * 2,
        out_specs=pl.BlockSpec(memory_space=pltpu.VMEM),
        scratch_shapes=[
            pltpu.VMEM((COLS, rows, width), jnp.bfloat16),
            pltpu.VMEM((COLS, width, width), jnp.bfloat16),
            pltpu.VMEM((rows, width), jnp.bfloat16),
            pltpu.VMEM((CHUNKS, BPC, part, BW), jnp.float32),
            pltpu.VMEM((CHUNKS, COLS, piece, width), jnp.bfloat16),
            pltpu.VMEM((CHUNKS, COLS, piece, width), jnp.bfloat16),
            pltpu.VMEM((CHUNKS, COLS, piece, width), jnp.bfloat16),
            dma,
            dma((COLS,)),
            dma((CHUNKS, 9)),
            dma((CHUNKS, 9)),
            dma((CHUNKS, 8)),
            dma((CHUNKS, 8)),
            dma((CHUNKS, COLS)),
            dma((CHUNKS, COLS)),
            dma((CHUNKS, COLS)),
            dma((CHUNKS, COLS)),
        ]
        + [pltpu.VMEM((COLS, piece, width), jnp.bfloat16)] * CHUNKS,
        compiler_params=pltpu.CompilerParams(
            collective_id=0, has_side_effects=True, vmem_limit_bytes=60 * 2**20
        ),
        name="ladder",
    )(block_irrep, irrep_size, partner, amplitudes, integrals)


def solution(mesh):
    in_specs = (P("row", "col"), P("col", None), P(), P(), P())
    return jax.shard_map(body, mesh=mesh, in_specs=in_specs, out_specs=P("row", "col"), check_vma=False)
```

time: 344 us -> 129 us (0.38)
  waiting for transfers between devices: 178 us -> 0 us
  Pallas kernels: 0 us -> 126 us
  local copies, waits for them, and re-layouts: 96.1 us -> 2.26 us
  matrix products: 29.8 us -> 0 us
  blocking collectives: 19.7 us -> 0 us
  between operations: 13.5 us -> 0.01 us
  other arithmetic: 5.35 us -> 0 us
    all_gather x2 -> x0, waiting for transfers between devices: 178 us -> none  [the longest x1 107 us: body(): everything = lax.all_gather(flipped, 'col', axis=1, tiled=True)]
    pallas_call x0 -> x1, Pallas kernels: none -> 126 us  [body(): pl.pallas_call(kernel, out_shape=jax.ShapeDtypeStruct((rows, width), jnp....]
    dot_general x1 -> x0, matrix products: 29.8 us -> none  [body(): lax.dot_general(lax.all_gather(masked_amp, 'col', axis=1, tiled=True), ma...]
    unnamed x5 -> x1, local copies, waits for them, and re-layouts: 31.2 us -> 2.26 us
    reshape x2 -> x0, local copies, waits for them, and re-layouts: 22.9 us -> none  [the longest x1 22.3 us: body(): everything.reshape(pair_rows, blocks, BW)]
    all_gather x1 -> x0, local copies, waits for them, and re-layouts: 22.4 us -> none  [body(): everything = lax.all_gather(flipped, 'col', axis=1, tiled=True)]
    all_to_all x1 -> x0, blocking collectives: 19.7 us -> none  [body(): lax.all_to_all(arranged, 'row', split_axis=1, concat_axis=1, tiled=True)]
    mul x1 -> x0, local copies, waits for them, and re-layouts: 11.1 us -> none  [body(): integrals.reshape(BPC, BW, blocks, BW) * allowed[:, None, :, None]]
  transfers between devices with their start and end apart: 2 -> 0, of which waited for: 2 -> 0; matrix products, arithmetic and copies ran while one was open for 13% -> 0% of each run, Pallas kernels for 0% -> 0%
where the time goes in v1:
time: 129 us
  Pallas kernels  126 us (98%)
  local copies, waits for them, and re-layouts  2.26 us (2%)
    pallas_call x1, Pallas kernels, body(): pl.pallas_call(kernel, out_shape=jax.ShapeDtypeStruct((rows, width), jnp....  126 us

profile of v1, /device:TPU:1, one launch (start us, length us, event | category | flops | bytes accessed | tf_op | source)
XLA Modules:
  0.0 128.6 jit_solution(4131911824304349220)
XLA Ops:
  0.0 126.3 %ladder.1 = bf16[512,1024]{1,0:T(8,128)(2,1)} custom-call(s32[64]{0:T(128)} %irrep.1, s32[4]{0:T(128)} %size.1, s32[64]{0:T(128)} %partner.1, bf16[512,1024]{1,0:T(8,128)(2,1)} %amp_hbm.1, bf16[1024,16384]{1,0:T(8,128)(2,1)} %int_hbm.1), custom_call_target="tpu_custom_call" | custom-call | tf_op jit(solution)/shard_map/ladder/pallas_call | solution.py:357
  126.3 2.3 %copy.7 = bf16[512,1024]{1,0:T(8,128)(2,1)} copy(bf16[512,1024]{1,0:T(8,128)(2,1)} %ladder.1) | data formatting | bytes 2097152

commit v2 on v1

v2 whole, which is shorter than its diff:
```python
import jax
import jax.numpy as jnp
from jax import lax
from jax.experimental import pallas as pl
from jax.experimental.pallas import tpu as pltpu
from jax.sharding import PartitionSpec as P

MESH = pl.DeviceIdType.MESH
BW = 256
BPC = 4
NOCC = 64
COLS = 16
ROWS = 8
FIRSTS = (4, 4)
CHUNKS = len(FIRSTS)


def one_hot(shape, target):
    row = lax.broadcasted_iota(jnp.int32, shape, 0)
    column = lax.broadcasted_iota(jnp.int32, shape, 1)
    return jnp.where(column == target(row), 1.0, 0.0).astype(jnp.bfloat16)


def kernel(irrep, size, partner, amp_hbm, int_hbm, out_ref, *scratch):
    (amp, ints, own, own_sem, int_sem, y_send, y_recv, k_send, k_recv, s1_send, s1_recv, s2_send, s2_recv, ready) = scratch[:14]
    total, ladder, recv1, send2, recv2 = (scratch[14 + n * CHUNKS : 14 + (n + 1) * CHUNKS] for n in range(5))
    rows, width = amp_hbm.shape
    parts = [f * NOCC for f in FIRSTS]
    begins = [sum(parts[:q]) for q in range(CHUNKS)]
    pieces = [p // COLS for p in parts]
    r, c = lax.axis_index("row"), lax.axis_index("col")
    y, zh, k = c // 4, (c // 2) % 2, c % 2

    def col(dy, dz, dk):
        return lax.rem(y + dy, 4) * 4 + lax.rem(zh + dz, 2) * 2 + lax.rem(k + dk, 2)

    up, down, across, twin = (r, col(1, 0, 0)), (r, col(3, 0, 0)), (r, col(0, 1, 0)), (r, col(0, 0, 1))

    def group_at(row, s):
        sy, sz, sk = s // 4, (s // 2) % 2, s % 2
        x, z = lax.rem(row % 4 + sy + 2 * sk, 4), lax.rem(row // 4 + sz, 2)
        return (z * 4 + x) * 2 + sk

    def sender(row, slot):
        there, sk = slot // 2, slot % 2
        sz = lax.rem(row // 4 + there // 4, 2)
        sy = lax.rem(row % 4 + 8 - there % 4 - 2 * sk, 4)
        return there, sy * 4 + sz * 2 + sk

    target = group_at(r, c) // 2
    origin = lax.rem(r // 4 + zh, 2) * 4 + lax.rem(r % 4 + 8 - y - 2 * k, 4)
    moves = target != r

    own_copy = pltpu.make_async_copy(amp_hbm, own, own_sem)
    own_copy.start()

    barrier = pltpu.get_barrier_semaphore()
    for to in (up, down, across, twin):
        pl.semaphore_signal(barrier, inc=1, device_id=to, device_id_type=MESH)

    @pl.when(moves)
    def _():
        pl.semaphore_signal(barrier, inc=1, device_id=(target, c), device_id_type=MESH)

    def int_copy(n):
        at = lax.rem(c + n, COLS)
        return pltpu.make_async_copy(
            int_hbm.at[:, pl.ds(pl.multiple_of(at * width, width), width)], ints.at[at], int_sem.at[at]
        )

    def live_of(base):
        lane = lax.broadcasted_iota(jnp.int32, (1, BW), 1)
        return jnp.concatenate(
            [jnp.where(lane < size[irrep[base + b]], 1.0, 0.0) for b in range(BPC)], axis=1
        )

    live = live_of(c * BPC)

    own_copy.wait()
    amp[c] = own[...] * live.astype(jnp.bfloat16)

    def start_int(n, carry):
        int_copy(n).start()
        return carry

    pl.semaphore_wait(barrier, jnp.where(moves, 5, 4))

    def move(at, q, start, count, to, sems, n):
        span = pl.ds(begins[q] + start, count)
        return pltpu.make_async_remote_copy(
            src_ref=amp.at[at, span], dst_ref=amp.at[at, span],
            send_sem=sems[0].at[q, n], recv_sem=sems[1].at[q, n],
            device_id=to, device_id_type=MESH,
        )

    ysem, ksem = (y_send, y_recv), (k_send, k_recv)
    started = []

    def go(copy):
        copy.start()
        started.append(copy)

    def send_own(q):
        go(move(c, q, 0, parts[q], up, ysem, 0))
        go(move(c, q, 0, parts[q], down, ysem, 1))
        go(move(c, q, 0, parts[q], across, ysem, 4))
        go(move(c, q, 0, parts[q], twin, ksem, 0))

    def arrived(at, q, start, count, sems, n):
        move(at, q, start, count, up, sems, n).wait_recv()

    def near(q):
        half = parts[q] // 2
        at = col(3, 0, 0)
        arrived(at, q, 0, parts[q], ysem, 0)
        go(move(at, q, 0, half, up, ysem, 2))
        go(move(at, q, half, half, across, ysem, 7))
        at = col(1, 0, 0)
        arrived(at, q, 0, parts[q], ysem, 1)
        go(move(at, q, half, half, down, ysem, 3))
        go(move(at, q, 0, half, across, ysem, 8))

    def near_twin(q):
        go(move(col(3, 0, 0), q, 0, parts[q], twin, ksem, 1))
        go(move(col(1, 0, 0), q, 0, parts[q], twin, ksem, 2))

    def over(q):
        half = parts[q] // 2
        at = col(0, 1, 0)
        arrived(at, q, 0, parts[q], ysem, 4)
        go(move(at, q, 0, half, up, ysem, 5))
        go(move(at, q, half, half, down, ysem, 6))
        go(move(at, q, 0, parts[q], twin, ksem, 3))

    def far(q):
        half = parts[q] // 2
        at = col(2, 0, 0)
        arrived(at, q, 0, half, ysem, 2)
        arrived(at, q, half, half, ysem, 3)
        go(move(at, q, 0, parts[q], twin, ksem, 4))

    def near_over(q):
        half = parts[q] // 2
        at = col(3, 1, 0)
        arrived(at, q, 0, half, ysem, 5)
        go(move(at, q, 0, half, up, ysem, 9))
        at = col(1, 1, 0)
        arrived(at, q, half, half, ysem, 6)
        go(move(at, q, half, half, down, ysem, 10))

    def near_over_twin(q):
        half = parts[q] // 2
        at = col(3, 1, 0)
        arrived(at, q, half, half, ysem, 7)
        go(move(at, q, 0, parts[q], twin, ksem, 5))
        at = col(1, 1, 0)
        arrived(at, q, 0, half, ysem, 8)
        go(move(at, q, 0, parts[q], twin, ksem, 6))

    def far_over(q):
        half = parts[q] // 2
        at = col(2, 1, 0)
        arrived(at, q, 0, half, ysem, 9)
        arrived(at, q, half, half, ysem, 10)
        go(move(at, q, 0, parts[q], twin, ksem, 7))

    def mask_ints(n, carry):
        int_copy(n).wait()
        at = lax.rem(c + n, COLS)
        for a in range(BPC):
            for b in range(BPC):
                same = irrep[c * BPC + a] == irrep[at * BPC + b]
                keep = jnp.where(same, 1.0, 0.0).astype(jnp.bfloat16)
                ints[at, a * BW : (a + 1) * BW, b * BW : (b + 1) * BW] *= keep
        return carry

    def multiply(q, at, first=False):
        product = lax.dot_general(
            ints[at], amp[at, begins[q] : begins[q] + parts[q], :],
            (((1,), (1,)), ((), ())), preferred_element_type=jnp.float32,
        )
        total[q][...] = product if first else total[q][...] + product

    def from_twin(q, n):
        dy, dz = ((0, 0), (3, 0), (1, 0), (0, 1), (2, 0), (3, 1), (1, 1), (2, 1))[n]
        at = col(dy, dz, 1)
        arrived(at, q, 0, parts[q], ksem, n)
        multiply(q, at)

    def row_ready():
        @pl.when(moves)
        def _():
            pl.semaphore_signal(ready, inc=1, device_id=(origin, c), device_id_type=MESH)

    def target_ready():
        @pl.when(moves)
        def _():
            pl.semaphore_wait(ready, 1)

    def step1(q, o):
        to = lax.rem(c + o, COLS)
        return pltpu.make_async_remote_copy(
            src_ref=ladder[q].at[group_at(r, to)], dst_ref=recv1[q].at[c], send_sem=s1_send.at[q, to], recv_sem=s1_recv.at[q, c],
            device_id=(r, to), device_id_type=MESH,
        )

    def exchange1(q):
        piece = pieces[q]

        def natural(n):
            group, rest = n // piece, n % piece
            return (rest // 4) * NOCC + group * 4 + rest % 4

        turned = lax.dot_general(
            one_hot((parts[q], parts[q]), natural), total[q][...].astype(jnp.bfloat16),
            (((1,), (1,)), ((), ())), preferred_element_type=jnp.float32,
        )
        ladder[q][...] = turned.astype(jnp.bfloat16).reshape(COLS, piece, width)

        def send(o, carry):
            step1(q, o).start()
            return carry

        lax.fori_loop(1, COLS, send, 0)
        recv1[q][c] = ladder[q][group_at(r, c)]

    def step2(q, to, slot):
        return pltpu.make_async_remote_copy(
            src_ref=send2[q].at[to], dst_ref=recv2[q].at[slot], send_sem=s2_send.at[q, to], recv_sem=s2_recv.at[q, slot],
            device_id=(target, to), device_id_type=MESH,
        )

    mine = r * 2 + k

    def exchange2(q):
        def arrive(o, carry):
            at = lax.rem(c + o, COLS)
            pltpu.make_async_remote_copy(
                src_ref=ladder[q].at[at], dst_ref=recv1[q].at[at], send_sem=s1_send.at[q, at], recv_sem=s1_recv.at[q, at],
                device_id=(r, at), device_id_type=MESH,
            ).wait_recv()
            return carry

        lax.fori_loop(1, COLS, arrive, 0)

        def send(o, carry):
            to = lax.rem(c + o, COLS)
            for b in range(BPC):
                source = partner[to * BPC + b] // BPC
                send2[q][to, :, b * BW : (b + 1) * BW] = recv1[q][source, :, b * BW : (b + 1) * BW]

            local = jnp.logical_and(target == r, to == c)

            @pl.when(jnp.logical_not(local))
            def _():
                step2(q, to, mine).start()

            @pl.when(local)
            def _():
                recv2[q][mine] = send2[q][to]

            return carry

        lax.fori_loop(0, COLS, send, 0)

    def exchange2_done(q):
        def arrive(slot, carry):
            there, column = sender(r, slot)

            @pl.when(jnp.logical_or(there != r, column != c))
            def _():
                step2(q, c, slot).wait_recv()

            return carry

        lax.fori_loop(0, 2 * ROWS, arrive, 0)

    send_own(0)
    lax.fori_loop(0, COLS, start_int, 0)
    lax.fori_loop(0, COLS, mask_ints, 0)
    multiply(0, c, first=True)
    near(0)
    over(0)
    send_own(1)
    near_twin(0)
    multiply(1, c, first=True)
    from_twin(0, 0)
    multiply(0, col(3, 0, 0))
    multiply(0, col(1, 0, 0))
    multiply(0, col(0, 1, 0))
    from_twin(0, 1)
    near_over(0)
    far(0)
    from_twin(0, 2)
    from_twin(0, 3)
    near(1)
    over(1)
    near_twin(1)
    near_over_twin(0)
    multiply(0, col(2, 0, 0))
    from_twin(0, 4)
    multiply(0, col(3, 1, 0))
    multiply(0, col(1, 1, 0))
    far_over(0)
    from_twin(0, 5)
    from_twin(0, 6)
    multiply(0, col(2, 1, 0))
    from_twin(0, 7)
    row_ready()
    exchange1(0)
    from_twin(1, 0)
    multiply(1, col(3, 0, 0))
    multiply(1, col(1, 0, 0))
    near_over(1)
    multiply(1, col(0, 1, 0))
    far(1)
    from_twin(1, 1)
    from_twin(1, 2)
    from_twin(1, 3)
    target_ready()
    exchange2(0)
    near_over_twin(1)
    multiply(1, col(2, 0, 0))
    from_twin(1, 4)
    multiply(1, col(3, 1, 0))
    multiply(1, col(1, 1, 0))
    far_over(1)
    from_twin(1, 5)
    from_twin(1, 6)
    multiply(1, col(2, 1, 0))
    from_twin(1, 7)
    exchange1(1)
    exchange2(1)
    exchange2_done(0)
    exchange2_done(1)
    for q in range(CHUNKS):
        piece = pieces[q]

        def grouped(m):
            first, second = m // NOCC, m % NOCC
            return (second // 4) * piece + first * 4 + second % 4

        result = jnp.dot(
            one_hot((parts[q], parts[q]), grouped), ladder[q][...].reshape(parts[q], width), preferred_element_type=jnp.float32
        )
        for p in range(CHUNKS):
            row = lax.broadcasted_iota(jnp.int32, (parts[q], parts[p]), 0)
            column = lax.broadcasted_iota(jnp.int32, (parts[q], parts[p]), 1)
            slot, rest = column // pieces[p], column % pieces[p]
            first = (slot % 2) * 4 + rest % 4
            second = (slot // 2) * ROWS + begins[p] // NOCC + rest // 4
            fetch = jnp.where(first * NOCC + second == row + begins[q], 1.0, 0.0).astype(jnp.bfloat16)
            result += jnp.dot(fetch, recv2[p][...].reshape(parts[p], width), preferred_element_type=jnp.float32)
        out_ref[begins[q] : begins[q] + parts[q], :] = (result * live).astype(jnp.bfloat16)

    for copy in started:
        copy.wait_send()
    for q in range(CHUNKS):

        def sent1(o, carry):
            step1(q, o).wait_send()
            return carry

        lax.fori_loop(1, COLS, sent1, 0)

        def sent2(to, carry):
            @pl.when(jnp.logical_not(jnp.logical_and(target == r, to == c)))
            def _():
                step2(q, to, mine).wait_send()

            return carry

        lax.fori_loop(0, COLS, sent2, 0)


def body(amplitudes, integrals, block_irrep, irrep_size, partner):
    rows, width = amplitudes.shape
    dma = pltpu.SemaphoreType.DMA
    held = [pltpu.VMEM((COLS, f * NOCC // COLS, width), jnp.bfloat16) for f in FIRSTS]
    return pl.pallas_call(
        kernel,
        out_shape=jax.ShapeDtypeStruct((rows, width), jnp.bfloat16),
        in_specs=[pl.BlockSpec(memory_space=pltpu.SMEM)] * 3 + [pl.BlockSpec(memory_space=pl.ANY)] * 2,
        out_specs=pl.BlockSpec(memory_space=pltpu.VMEM),
        scratch_shapes=[
            pltpu.VMEM((COLS, rows, width), jnp.bfloat16),
            pltpu.VMEM((COLS, width, width), jnp.bfloat16),
            pltpu.VMEM((rows, width), jnp.bfloat16),
            dma,
            dma((COLS,)),
            dma((CHUNKS, 11)),
            dma((CHUNKS, 11)),
            dma((CHUNKS, 8)),
            dma((CHUNKS, 8)),
            dma((CHUNKS, COLS)),
            dma((CHUNKS, COLS)),
            dma((CHUNKS, COLS)),
            dma((CHUNKS, COLS)),
            pltpu.SemaphoreType.REGULAR,
        ]
        + [pltpu.VMEM((width, f * NOCC), jnp.float32) for f in FIRSTS]
        + held * 4,
        compiler_params=pltpu.CompilerParams(
            collective_id=0, has_side_effects=True, vmem_limit_bytes=58 * 2**20
        ),
        name="ladder",
    )(block_irrep, irrep_size, partner, amplitudes, integrals)


def solution(mesh):
    in_specs = (P("row", "col"), P("col", None), P(), P(), P())
    return jax.shard_map(body, mesh=mesh, in_specs=in_specs, out_specs=P("row", "col"), check_vma=False)
```

time: 129 us -> 106 us (0.82)
  Pallas kernels: 126 us -> 104 us
    pallas_call x1, Pallas kernels: 126 us -> 104 us  [body(): pl.pallas_call(kernel, out_shape=jax.ShapeDtypeStruct((rows, width), jnp....]
where the time goes in v2:
time: 106 us
  Pallas kernels  104 us (98%)
  local copies, waits for them, and re-layouts  2.26 us (2%)
    pallas_call x1, Pallas kernels, body(): pl.pallas_call(kernel, out_shape=jax.ShapeDtypeStruct((rows, width), jnp....  104 us
    unnamed x1, local copies, waits for them, and re-layouts  2.26 us

profile of v2, /device:TPU:1, one launch (start us, length us, event | category | flops | bytes accessed | tf_op | source)
XLA Modules:
  0.0 106.2 jit_solution(17472348216497699381)
XLA Ops:
  0.0 103.9 %ladder.1 = bf16[512,1024]{1,0:T(8,128)(2,1)} custom-call(s32[64]{0:T(128)} %irrep.1, s32[4]{0:T(128)} %size.1, s32[64]{0:T(128)} %partner.1, bf16[512,1024]{1,0:T(8,128)(2,1)} %amp_hbm.1, bf16[1024,16384]{1,0:T(8,128)(2,1)} %int_hbm.1), custom_call_target="tpu_custom_call" | custom-call | tf_op jit(solution)/shard_map/ladder/pallas_call | solution.py:380
  103.9 2.3 %copy.7 = bf16[512,1024]{1,0:T(8,128)(2,1)} copy(bf16[512,1024]{1,0:T(8,128)(2,1)} %ladder.1) | data formatting | bytes 2097152

commit v3 on v2

--- a/solution.py
+++ b/solution.py
@@ -22,8 +22,8 @@
 
 
 def kernel(irrep, size, partner, amp_hbm, int_hbm, out_ref, *scratch):
-    (amp, ints, own, own_sem, int_sem, y_send, y_recv, k_send, k_recv, s1_send, s1_recv, s2_send, s2_recv, ready) = scratch[:14]
-    total, ladder, recv1, send2, recv2 = (scratch[14 + n * CHUNKS : 14 + (n + 1) * CHUNKS] for n in range(5))
+    (amp, ints, own_sem, int_sem, y_send, y_recv, k_send, k_recv, s1_send, s1_recv, s2_send, s2_recv, ready) = scratch[:13]
+    total, ladder, recv1, send2, recv2 = (scratch[13 + n * CHUNKS : 13 + (n + 1) * CHUNKS] for n in range(5))
     rows, width = amp_hbm.shape
     parts = [f * NOCC for f in FIRSTS]
     begins = [sum(parts[:q]) for q in range(CHUNKS)]
@@ -51,7 +51,7 @@
     origin = lax.rem(r // 4 + zh, 2) * 4 + lax.rem(r % 4 + 8 - y - 2 * k, 4)
     moves = target != r
 
-    own_copy = pltpu.make_async_copy(amp_hbm, own, own_sem)
+    own_copy = pltpu.make_async_copy(amp_hbm, amp.at[c], own_sem)
     own_copy.start()
 
     barrier = pltpu.get_barrier_semaphore()
@@ -77,7 +77,7 @@
     live = live_of(c * BPC)
 
     own_copy.wait()
-    amp[c] = own[...] * live.astype(jnp.bfloat16)
+    amp[c] *= live.astype(jnp.bfloat16)
 
     def start_int(n, carry):
         int_copy(n).start()
@@ -132,21 +132,25 @@
         go(move(at, q, half, half, down, ysem, 6))
         go(move(at, q, 0, parts[q], twin, ksem, 3))
 
+    def edge(q):
+        return parts[q] * 5 // 16
+
     def far(q):
         half = parts[q] // 2
         at = col(2, 0, 0)
         arrived(at, q, 0, half, ysem, 2)
         arrived(at, q, half, half, ysem, 3)
+        go(move(at, q, edge(q), parts[q] - 2 * edge(q), across, ysem, 11))
         go(move(at, q, 0, parts[q], twin, ksem, 4))
 
     def near_over(q):
         half = parts[q] // 2
         at = col(3, 1, 0)
         arrived(at, q, 0, half, ysem, 5)
-        go(move(at, q, 0, half, up, ysem, 9))
+        go(move(at, q, 0, edge(q), up, ysem, 9))
         at = col(1, 1, 0)
         arrived(at, q, half, half, ysem, 6)
-        go(move(at, q, half, half, down, ysem, 10))
+        go(move(at, q, parts[q] - edge(q), edge(q), down, ysem, 10))
 
     def near_over_twin(q):
         half = parts[q] // 2
@@ -158,10 +162,10 @@
         go(move(at, q, 0, parts[q], twin, ksem, 6))
 
     def far_over(q):
-        half = parts[q] // 2
         at = col(2, 1, 0)
-        arrived(at, q, 0, half, ysem, 9)
-        arrived(at, q, half, half, ysem, 10)
+        arrived(at, q, 0, edge(q), ysem, 9)
+        arrived(at, q, parts[q] - edge(q), edge(q), ysem, 10)
+        arrived(at, q, edge(q), parts[q] - 2 * edge(q), ysem, 11)
         go(move(at, q, 0, parts[q], twin, ksem, 7))
 
     def mask_ints(n, carry):
@@ -379,17 +383,16 @@
     held = [pltpu.VMEM((COLS, f * NOCC // COLS, width), jnp.bfloat16) for f in FIRSTS]
     return pl.pallas_call(
         kernel,
-        out_shape=jax.ShapeDtypeStruct((rows, width), jnp.bfloat16),
+        out_shape=pltpu.VMEM((rows, width), jnp.bfloat16),
         in_specs=[pl.BlockSpec(memory_space=pltpu.SMEM)] * 3 + [pl.BlockSpec(memory_space=pl.ANY)] * 2,
         out_specs=pl.BlockSpec(memory_space=pltpu.VMEM),
         scratch_shapes=[
             pltpu.VMEM((COLS, rows, width), jnp.bfloat16),
             pltpu.VMEM((COLS, width, width), jnp.bfloat16),
-            pltpu.VMEM((rows, width), jnp.bfloat16),
             dma,
             dma((COLS,)),
-            dma((CHUNKS, 11)),
-            dma((CHUNKS, 11)),
+            dma((CHUNKS, 12)),
+            dma((CHUNKS, 12)),
             dma((CHUNKS, 8)),
             dma((CHUNKS, 8)),
             dma((CHUNKS, COLS)),
@@ -401,7 +404,7 @@
         + [pltpu.VMEM((width, f * NOCC), jnp.float32) for f in FIRSTS]
         + held * 4,
         compiler_params=pltpu.CompilerParams(
-            collective_id=0, has_side_effects=True, vmem_limit_bytes=58 * 2**20
+            collective_id=0, has_side_effects=True, vmem_limit_bytes=57 * 2**20
         ),
         name="ladder",
     )(block_irrep, irrep_size, partner, amplitudes, integrals)

time: 106 us -> 102 us (0.962)
  Pallas kernels: 104 us -> 101 us
  local copies, waits for them, and re-layouts: 2.26 us -> 0.97 us
    pallas_call x1, Pallas kernels: 104 us -> 101 us  [body(): pl.pallas_call(kernel, out_shape=pltpu.VMEM((rows, width), jnp.bfloat16),...]
    unnamed x1, local copies, waits for them, and re-layouts: 2.26 us -> 0.97 us
where the time goes in v3:
time: 102 us
  Pallas kernels  101 us (99%)
    pallas_call x1, Pallas kernels, body(): pl.pallas_call(kernel, out_shape=pltpu.VMEM((rows, width), jnp.bfloat16),...  101 us

profile of v3, /device:TPU:1, one launch (start us, length us, event | category | flops | bytes accessed | tf_op | source)
XLA Modules:
  0.0 101.8 jit_solution(1690152340699508018)
XLA Ops:
  0.0 100.9 %ladder.1 = bf16[512,1024]{1,0:T(8,128)(2,1)S(1)} custom-call(s32[64]{0:T(128)} %irrep.1, s32[4]{0:T(128)} %size.1, s32[64]{0:T(128)} %partner.1, bf16[512,1024]{1,0:T(8,128)(2,1)} %amp_hbm.1, bf16[1024,16384]{1,0:T(8,128)(2,1)} %int_hbm.1), custom_call_target="tpu_custom_call" | custom-call | tf_op jit(solution)/shard_map/ladder/pallas_call | solution.py:384
  100.9 1.0 copy.7

commit v4 on v3

--- a/solution.py
+++ b/solution.py
@@ -24,6 +24,7 @@
 def kernel(irrep, size, partner, amp_hbm, int_hbm, out_ref, *scratch):
     (amp, ints, own_sem, int_sem, y_send, y_recv, k_send, k_recv, s1_send, s1_recv, s2_send, s2_recv, ready) = scratch[:13]
     total, ladder, recv1, send2, recv2 = (scratch[13 + n * CHUNKS : 13 + (n + 1) * CHUNKS] for n in range(5))
+    partial, ones = scratch[13 + 5 * CHUNKS : 13 + 6 * CHUNKS], scratch[13 + 6 * CHUNKS :]
     rows, width = amp_hbm.shape
     parts = [f * NOCC for f in FIRSTS]
     begins = [sum(parts[:q]) for q in range(CHUNKS)]
@@ -293,8 +294,8 @@
     multiply(0, col(1, 0, 0))
     multiply(0, col(0, 1, 0))
     from_twin(0, 1)
+    far(0)
     near_over(0)
-    far(0)
     from_twin(0, 2)
     from_twin(0, 3)
     near(1)
@@ -316,8 +317,8 @@
     multiply(1, col(3, 0, 0))
     multiply(1, col(1, 0, 0))
     near_over(1)
+    far(1)
     multiply(1, col(0, 1, 0))
-    far(1)
     from_twin(1, 1)
     from_twin(1, 2)
     from_twin(1, 3)
@@ -335,8 +336,14 @@
     from_twin(1, 7)
     exchange1(1)
     exchange2(1)
-    exchange2_done(0)
-    exchange2_done(1)
+    def fetch(q, p):
+        row = lax.broadcasted_iota(jnp.int32, (parts[q], parts[p]), 0)
+        column = lax.broadcasted_iota(jnp.int32, (parts[q], parts[p]), 1)
+        slot, rest = column // pieces[p], column % pieces[p]
+        first = (slot % 2) * 4 + rest % 4
+        second = (slot // 2) * ROWS + begins[p] // NOCC + rest // 4
+        return jnp.where(first * NOCC + second == row + begins[q], 1.0, 0.0).astype(jnp.bfloat16)
+
     for q in range(CHUNKS):
         piece = pieces[q]
 
@@ -347,14 +354,17 @@
         result = jnp.dot(
             one_hot((parts[q], parts[q]), grouped), ladder[q][...].reshape(parts[q], width), preferred_element_type=jnp.float32
         )
-        for p in range(CHUNKS):
-            row = lax.broadcasted_iota(jnp.int32, (parts[q], parts[p]), 0)
-            column = lax.broadcasted_iota(jnp.int32, (parts[q], parts[p]), 1)
-            slot, rest = column // pieces[p], column % pieces[p]
-            first = (slot % 2) * 4 + rest % 4
-            second = (slot // 2) * ROWS + begins[p] // NOCC + rest // 4
-            fetch = jnp.where(first * NOCC + second == row + begins[q], 1.0, 0.0).astype(jnp.bfloat16)
-            result += jnp.dot(fetch, recv2[p][...].reshape(parts[p], width), preferred_element_type=jnp.float32)
+        if q == 0:
+            exchange2_done(0)
+        partial[q][...] = result + jnp.dot(
+            fetch(q, 0), recv2[0][...].reshape(parts[0], width), preferred_element_type=jnp.float32
+        )
+        ones[q][...] = fetch(q, 1)
+    exchange2_done(1)
+    for q in range(CHUNKS):
+        result = partial[q][...] + jnp.dot(
+            ones[q][...], recv2[1][...].reshape(parts[1], width), preferred_element_type=jnp.float32
+        )
         out_ref[begins[q] : begins[q] + parts[q], :] = (result * live).astype(jnp.bfloat16)
 
     for copy in started:
@@ -402,9 +412,11 @@
             pltpu.SemaphoreType.REGULAR,
         ]
         + [pltpu.VMEM((width, f * NOCC), jnp.float32) for f in FIRSTS]
-        + held * 4,
+        + held * 4
+        + [pltpu.VMEM((f * NOCC, width), jnp.float32) for f in FIRSTS]
+        + [pltpu.VMEM((f * NOCC, FIRSTS[1] * NOCC), jnp.bfloat16) for f in FIRSTS],
         compiler_params=pltpu.CompilerParams(
-            collective_id=0, has_side_effects=True, vmem_limit_bytes=57 * 2**20
+            collective_id=0, has_side_effects=True, vmem_limit_bytes=59 * 2**20
         ),
         name="ladder",
     )(block_irrep, irrep_size, partner, amplitudes, integrals)

time: 102 us -> 101 us (level)
  no operation moved by 1% of the time
where the time goes in v4:
time: 101 us
  Pallas kernels  100 us (99%)
    pallas_call x1, Pallas kernels, body(): pl.pallas_call(kernel, out_shape=pltpu.VMEM((rows, width), jnp.bfloat16),...  100 us

profile of v4, /device:TPU:1, one launch (start us, length us, event | category | flops | bytes accessed | tf_op | source)
XLA Modules:
  0.0 101.2 jit_solution(17615845009245542897)
XLA Ops:
  0.0 100.3 %ladder.1 = bf16[512,1024]{1,0:T(8,128)(2,1)S(1)} custom-call(s32[64]{0:T(128)} %irrep.1, s32[4]{0:T(128)} %size.1, s32[64]{0:T(128)} %partner.1, bf16[512,1024]{1,0:T(8,128)(2,1)} %amp_hbm.1, bf16[1024,16384]{1,0:T(8,128)(2,1)} %int_hbm.1), custom_call_target="tpu_custom_call" | custom-call | tf_op jit(solution)/shard_map/ladder/pallas_call | solution.py:394
  100.3 1.0 copy.7
